TPU v7x, 32 devices: a whole 2x2x4 slice. The times are simulated.
32 devices in a mesh: dp: 2 (over x), seq: 16 (over z, y, core).
Axes of the slice: x: 2, y: 2, z: 4, core: 2. Of those that a mesh axis runs over, the one named last changes fastest.
Arguments:
- tokens: bfloat16 [2, 2048, 1536], P('dp', 'seq'), may hold values from -6 to 6
- query_weight: bfloat16 [1536, 1024], P('seq'), may hold values from -0.15564466 to 0.15564466
- key_weight: bfloat16 [1536, 128], P('seq'), may hold values from -7.6546554 to 7.6546554
- value_weight: bfloat16 [1536, 128], P('seq'), may hold values from -0.15625 to 0.15625
- output_weight: bfloat16 [1536, 1024], P('seq'), may hold values from -0.1875 to 0.1875
- row_weight: bfloat16 [1536, 128], replicated, may hold values from -0.15625 to 0.15625
- col_weight: bfloat16 [1536, 128], replicated, may hold values from -0.15625 to 0.15625
- pair_cotangent: bfloat16 [2, 128, 128, 128], P('dp', 'seq'), may hold values from -0.046875 to 0.046875
Outputs:
- pair: bfloat16 [2, 128, 128, 128], P('dp', 'seq')
- grad_row_weight: bfloat16 [1536, 128], replicated
- grad_col_weight: bfloat16 [1536, 128], replicated
All inputs are finite; a program needn't handle non-finite values.
Results may differ from a plain program's by a relative error of at most 0.025.
The roundings to bfloat16 on the way count: a program that leaves them out, or rounds other values in their place, can miss the bound.
Values may be sent and summed in bfloat16 or wider, within the bound.
A program may use at most 64 MiB of HBM per device.

v0:
```python
import math

import jax
import jax.numpy as jnp
from jax import lax
from jax.sharding import PartitionSpec as P

POOL = 16


def rms_rows(values):
    return values * lax.rsqrt(jnp.mean(values * values, axis=-1, keepdims=True) + 1e-06)


def attend_block(carry, query_rows, key_block, value_block, scale):
    run_max, run_total, run_acc = carry
    scores = jnp.dot(query_rows, key_block.T, preferred_element_type=jnp.float32) * scale
    new_max = jnp.maximum(run_max, jnp.max(scores, axis=1))
    weights = jnp.exp(scores - new_max[:, None])
    factor = jnp.exp(run_max - new_max)
    run_total = run_total * factor + jnp.sum(weights, axis=1)
    rounded = weights.astype(jnp.bfloat16)
    run_acc = run_acc * factor[:, None] + jnp.dot(
        rounded, value_block, preferred_element_type=jnp.float32
    )
    return (new_max, run_total, run_acc)


def on_device(
    tokens,
    query_weight,
    key_weight,
    value_weight,
    output_weight,
    row_weight,
    col_weight,
    pair_cotangent,
):
    tok_rows = tokens.shape[1]
    width = tokens.shape[2]
    head_size = key_weight.shape[1]
    heads_wide = query_weight.shape[1]
    heads_count = heads_wide // head_size
    normed = rms_rows(tokens[0].astype(jnp.float32)).astype(jnp.bfloat16)
    pieces = (
        lax.all_gather(query_weight, "seq", axis=0, tiled=True),
        lax.all_gather(key_weight, "seq", axis=0, tiled=True),
        lax.all_gather(value_weight, "seq", axis=0, tiled=True),
    )
    q_sum, k_sum, v_sum = tuple(
        (jnp.dot(normed, piece, preferred_element_type=jnp.float32) for piece in pieces)
    )
    queries = q_sum.astype(jnp.bfloat16)
    keys = k_sum.astype(jnp.bfloat16)
    values = v_sum.astype(jnp.bfloat16)
    query_rows = queries.reshape(tok_rows * heads_count, head_size)
    scale = 1.0 / math.sqrt(head_size)
    row_count = tok_rows * heads_count
    start_state = (
        jnp.full((row_count,), -1e30, jnp.float32),
        jnp.zeros((row_count,), jnp.float32),
        jnp.zeros((row_count, head_size), jnp.float32),
    )
    carry = start_state
    key_piece = lax.all_gather(keys, "seq", axis=0, tiled=True)
    value_piece = lax.all_gather(values, "seq", axis=0, tiled=True)
    count = key_piece.shape[0]
    key_stack = key_piece.reshape(count // 512, 512, head_size)
    value_stack = value_piece.reshape(count // 512, 512, head_size)

    def step_block(state, blocks):
        return (attend_block(state, query_rows, blocks[0], blocks[1], scale), None)

    carry, unused = lax.scan(step_block, carry, (key_stack, value_stack))
    run_max, run_total, run_acc = carry
    attended = (run_acc / run_total[:, None]).astype(jnp.bfloat16).reshape(tok_rows, heads_wide)
    contract_last = (((1,), (1,)), ((), ()))
    update = lax.dot_general(
        attended,
        lax.all_gather(output_weight, "seq", axis=0, tiled=True),
        contract_last,
        preferred_element_type=jnp.float32,
    )
    bin_rows = tok_rows // POOL
    pooled = jnp.mean(update.reshape(bin_rows, POOL, width), axis=1)
    bin_feat = rms_rows(pooled).astype(jnp.bfloat16)
    row_proj = jnp.dot(bin_feat, row_weight, preferred_element_type=jnp.float32).astype(
        jnp.bfloat16
    )
    col_proj = jnp.dot(
        lax.all_gather(bin_feat, "seq", axis=0, tiled=True),
        col_weight,
        preferred_element_type=jnp.float32,
    ).astype(jnp.bfloat16)
    pair = (
        row_proj.astype(jnp.float32)[:, None, :] * col_proj.astype(jnp.float32)[None, :, :]
    ).astype(jnp.bfloat16)
    cotangent = pair_cotangent[0]
    row_grad = jnp.einsum(
        "ijc,jc->ic", cotangent, col_proj, preferred_element_type=jnp.float32
    ).astype(jnp.bfloat16)
    col_terms = jnp.einsum("ijc,ic->jc", cotangent, row_proj, preferred_element_type=jnp.float32)
    col_grad = lax.psum_scatter(col_terms, "seq", scatter_dimension=0, tiled=True).astype(
        jnp.bfloat16
    )
    contract_first = (((0,), (0,)), ((), ()))
    grad_row = lax.dot_general(
        bin_feat, row_grad, contract_first, preferred_element_type=jnp.float32
    )
    grad_col = lax.dot_general(
        bin_feat, col_grad, contract_first, preferred_element_type=jnp.float32
    )
    grad_row, grad_col = lax.psum((grad_row, grad_col), ("dp", "seq"))
    return (pair[None], grad_row.astype(jnp.bfloat16), grad_col.astype(jnp.bfloat16))


def solution(mesh):
    placed = (
        P("dp", "seq", None),
        P("seq", None),
        P("seq", None),
        P("seq", None),
        P("seq", None),
        P(),
        P(),
        P("dp", "seq", None, None),
    )
    return jax.shard_map(
        on_device,
        mesh=mesh,
        in_specs=placed,
        out_specs=(P("dp", "seq", None, None), P(), P()),
        check_vma=False,
    )
```

profile of v0, /device:TPU:0, one launch (start us, length us, event | category | flops | bytes accessed | tf_op | source)
XLA Modules:
  0.0 261.0 jit_solution(14288850674625973761)
XLA Ops:
  7.2 0.0 copy-start
  7.2 0.0 copy-start.5
  7.2 0.0 copy-start.1
  7.2 0.0 copy-start.4
  7.2 0.0 all-gather.3.cloned.1.call-start
  7.3 0.7 all-gather.3.cloned.1.call-update
  7.9 0.0 all-gather.5.cloned.1.call-start
  8.0 0.7 all-gather.5.cloned.1.call-update
  8.7 1.2 fusion.19
  9.9 24.8 %all_gather.21 = bf16[1536,128]{1,0:T(8,128)(2,1)S(1)} all-gather(bf16[96,128]{1,0:T(8,128)(2,1)} %param.12), channel_id=1, replica_groups=mesh['dp'=2,'seq'=16] {'seq'}, dimensions={0}, use_global_device_ids=true | all-gather | bytes 417792 | tf_op jit(solution)/shard_map/all_gather | solution.py:47
  34.7 1.3 convolution_convert_fusion.3
  36.0 21.2 %all_gather.22 = bf16[2048,128]{1,0:T(8,128)(2,1)} all-gather(bf16[128,128]{1,0:T(8,128)(2,1)S(1)} %convolution_convert_fusion.3), channel_id=1, replica_groups=mesh['dp'=2,'seq'=16] {'seq'}, dimensions={0}, use_global_device_ids=true | all-gather | bytes 557056 | tf_op jit(solution)/shard_map/all_gather | solution.py:65
  57.2 0.0 copy-done.4
  57.2 20.1 %all_gather.24 = bf16[1536,128]{1,0:T(8,128)(2,1)S(1)} all-gather(bf16[96,128]{1,0:T(8,128)(2,1)S(1)} %copy-done.4), channel_id=1, replica_groups=mesh['dp'=2,'seq'=16] {'seq'}, dimensions={0}, use_global_device_ids=true | all-gather | bytes 417792 | tf_op jit(solution)/shard_map/all_gather | solution.py:48
  77.2 0.0 copy-done.1
  77.2 0.3 convolution_convert_fusion.2
  77.6 0.0 copy-done.5
  77.6 0.6 dynamic-slice
  78.8 21.8 %all_gather.25 = bf16[2048,128]{1,0:T(8,128)(2,1)} all-gather(bf16[128,128]{1,0:T(8,128)(2,1)S(1)} %convolution_convert_fusion.2), channel_id=1, replica_groups=mesh['dp'=2,'seq'=16] {'seq'}, dimensions={0}, use_global_device_ids=true | all-gather | bytes 557056 | tf_op jit(solution)/shard_map/all_gather | solution.py:66
  100.6 0.0 all-gather.3.cloned.1.call-done
  100.6 2.5 convolution_convert_fusion
  103.1 0.1 reshape.49
  103.2 13.3 %while.15 = (s32[]{:T(128)}, f32[1024]{0:T(1024)S(1)}, f32[1024]{0:T(1024)S(1)}, f32[1024,128]{1,0:T(8,128)S(1)}, bf16[4,512,128]{2,1,0:T(8,128)(2,1)}, /*index=...) while((s32[]{:T(128)}, f32[1024]{0:T(1024)S(1)}, ...), condition=%wide.region_4.5_spmd.clone, body=%wide.region_1.4_spmd.clone.sunk | while | flops 273028096 | bytes 7930985 | solution.py:74
  103.3 1.3 multiply_reduce_fusion.5
  104.6 0.4 fusion.49
  105.0 1.5 convolution_add_fusion.2
  106.6 1.3 multiply_reduce_fusion.5
  108.0 0.4 fusion.49
  108.3 1.6 convolution_add_fusion.2
  109.9 1.3 multiply_reduce_fusion.5
  111.3 0.4 fusion.49
  111.7 1.5 convolution_add_fusion.2
  113.3 1.3 multiply_reduce_fusion.5
  114.6 0.4 fusion.49
  115.0 1.5 convolution_add_fusion.2
  116.6 0.2 divide_convert_fusion
  116.8 0.1 dot_general.41
  116.9 0.0 copy-start.3
  116.9 0.0 copy-start.2
  117.0 0.0 all-gather.5.cloned.1.call-done
  117.0 3.1 %fusion.16 = f32[8,1536]{1,0:T(8,128)S(1)} fusion(bf16[8,16,1024]{2,1,0:T(8,128)(2,1)S(1)} %dot_general.41, bf16[1536,1024]{1,0:T(8,128)(2,1)} %all-gather.5.cloned.1.call-done), kind=kOutput, calls=%fused_computation.22 | convolution fusion | flops 402837504 | bytes 3457024 | tf_op jit(solution)/shard_map/dot_general | solution.py:78
  120.1 0.1 multiply_reduce_fusion.3
  120.3 0.1 multiply_convert_fusion.1
  120.3 19.8 %all_gather.27 = bf16[128,1536]{1,0:T(8,128)(2,1)S(1)} all-gather(bf16[8,1536]{1,0:T(8,128)(2,1)S(1)} %multiply_convert_fusion.1), channel_id=1, replica_groups=mesh['dp'=2,'seq'=16] {'seq'}, dimensions={0}, use_global_device_ids=true | all-gather | bytes 417792 | tf_op jit(solution)/shard_map/all_gather | solution.py:91
  140.1 0.0 copy-done.3
  140.1 0.2 bitcast_convert_fusion.1
  140.3 0.0 copy-done.2
  140.3 0.1 multiply_reduce_fusion.1
  140.3 0.1 copy.24
  140.4 57.9 %all-reduce = bf16[128,128]{0,1:T(8,128)(2,1)S(1)} all-reduce(f32[128,128]{0,1:T(8,128)S(1)} %bitcast.57), channel_id=2, replica_groups=mesh['dp'=2,'seq'=16] {'seq'}, use_global_device_ids=true, to_apply=%region_8.9.clone | all-reduce | flops 16384 | bytes 98304
  198.4 0.4 fusion.21
  198.7 0.0 copy-done
  198.7 0.3 bitcast_convert_fusion
  199.0 0.1 multiply_reduce_fusion.2
  199.1 0.1 copy.17
  199.2 0.3 fusion.28
  199.5 53.9 %all-reduce.3 = (bf16[1536,128]{1,0:T(8,128)(2,1)}, bf16[1536,128]{1,0:T(8,128)(2,1)}) all-reduce(f32[1536,128]{1,0:T(8,128)S(1)} %fusion.28, f32[1536,128]{1,0:T(8,128)S(1)} %fusion.21), channel_id=1, replica_groups=mesh['dp'=2,'seq'=16] {'dp','seq'}, use_global_device_ids=true, to_apply=%region_7.8 | all-reduce | flops 393216 | bytes 2359296 | tf_op jit(solution)/shard_map/psum | solution.py:113
  253.4 0.8 multiply_convert_fusion
  (17 shorter events, 0.1 us)
Async XLA Ops:
  7.2 191.6 %copy-start = (bf16[1536,128]{1,0:T(8,128)(2,1)S(1)}, bf16[1536,128]{1,0:T(8,128)(2,1)}, u32[]{:S(2)}) copy-start(bf16[1536,128]{1,0:T(8,128)(2,1)} %param.16) | copy-start | bytes 1179652
  7.2 70.4 %copy-start.5 = (u32[32]{0:T(128)S(1)}, u32[32]{0:T(128)}, u32[]{:S(2)}) copy-start(u32[32]{0:T(128)} %constant.39) | copy-start | bytes 388
  7.2 70.0 %copy-start.1 = (bf16[1,128,1536]{2,1,0:T(8,128)(2,1)S(1)}, bf16[1,128,1536]{2,1,0:T(8,128)(2,1)}, u32[]{:S(2)}) copy-start(bf16[1,128,1536]{2,1,0:T(8,128)(2,1)} %param.10) | copy-start | bytes 1179652
  7.2 50.0 %copy-start.4 = (bf16[96,128]{1,0:T(8,128)(2,1)S(1)}, bf16[96,128]{1,0:T(8,128)(2,1)}, u32[]{:S(2)}) copy-start(bf16[96,128]{1,0:T(8,128)(2,1)} %param.13) | copy-start | bytes 73732
  7.2 93.4 %all-gather.3.cloned.1.call-start = ((), (), s32[]{:S(2)}) async-start(), calls=%async_computation | async-start | bytes 3342336 | tf_op jit(solution)/shard_map/all_gather | solution.py:46
  7.9 109.0 %all-gather.5.cloned.1.call-start = ((), (), s32[]{:S(2)}) async-start(), calls=%async_computation.1 | async-start | bytes 3342336 | tf_op jit(solution)/shard_map/all_gather | solution.py:80
  116.9 23.2 %copy-start.3 = (bf16[1536,128]{1,0:T(8,128)(2,1)S(1)}, bf16[1536,128]{1,0:T(8,128)(2,1)}, u32[]{:S(2)}) copy-start(bf16[1536,128]{1,0:T(8,128)(2,1)} %param.15) | copy-start | bytes 1179652
  116.9 23.3 %copy-start.2 = (bf16[1,8,128,128]{3,2,1,0:T(8,128)(2,1)S(1)}, bf16[1,8,128,128]{3,2,1,0:T(8,128)(2,1)}, u32[]{:S(2)}) copy-start(bf16[1,8,128,128]{3,2,1,0:T(8,128)(2,1)} %param.17) | copy-start | bytes 786436
Sparse Core Ops, SparseCore 0:
  10.3 50.6 all-gather.2
  63.3 46.2 all-gather.4
where the time goes:
time: 261 us
  blocking collectives  219 us (84%)
  matrix products  19.9 us (8%)
  between operations  14.9 us (6%)
  other arithmetic  4.03 us (2%)
    unnamed x1, blocking collectives  57.9 us
    psum x1, blocking collectives, on_device(): grad_row, grad_col = lax.psum((grad_row, grad_col), ('dp', 'seq'))  53.9 us
    all_gather x1, blocking collectives, on_device(): lax.all_gather(key_weight, 'seq', axis=0, tiled=True)  24.8 us
    all_gather x1, blocking collectives, on_device(): value_piece = lax.all_gather(values, 'seq', axis=0, tiled=True)  21.8 us
    all_gather x1, blocking collectives, on_device(): key_piece = lax.all_gather(keys, 'seq', axis=0, tiled=True)  21.2 us
    all_gather x1, blocking collectives, on_device(): lax.all_gather(value_weight, 'seq', axis=0, tiled=True)  20.1 us
    all_gather x1, blocking collectives, on_device(): lax.all_gather(bin_feat, 'seq', axis=0, tiled=True)  19.8 us
    dot_general x4, matrix products, attend_block(): jnp.dot(rounded, value_block, preferred_element_type=jnp.float32)  6.17 us
  transfers between devices with their start and end apart: 2, of which 0 were waited for; matrix products, arithmetic and copies ran while one was open for 7% of the time, Pallas kernels for 0%

commit v1 on v0

v1 whole, which is shorter than its diff:
```python
import functools
import math

import jax
import jax.numpy as jnp
from jax import lax
from jax.experimental import pallas as pl
from jax.experimental.pallas import tpu as pltpu
from jax.sharding import PartitionSpec as P

POOL = 16
LINE = 4
F32 = jnp.float32
BF16 = jnp.bfloat16
MESH = pl.DeviceIdType.MESH
LAST = (((1,), (1,)), ((), ()))


def merge_rows(block, rows):
    if block.shape[1] % 16 == 0:
        return block.reshape(rows, block.shape[2])
    return block.astype(F32).reshape(rows, block.shape[2]).astype(block.dtype)


class Where:
    def __init__(self, n_dp, n_seq):
        self.n_dp, self.n_seq = n_dp, n_seq
        self.mid = n_seq // (LINE * 2)
        self.dp, self.me = lax.axis_index("dp"), lax.axis_index("seq")
        self.core = self.me % 2
        self.y = (self.me // 2) % self.mid
        self.z = self.me // (2 * self.mid)

    def at(self, dz, dy, flip):
        z = (self.z + dz) % LINE
        y = (self.y + dy) % self.mid
        core = 1 - self.core if flip else self.core
        return (z * self.mid + y) * 2 + core

    def near(self):
        return (
            [self.at(dz, 0, False) for dz in range(1, LINE)]
            + [self.at(0, dy, False) for dy in range(1, self.mid)]
            + [self.at(0, 0, True)]
        )


class Gather:
    def __init__(self, where, slot, send_sem, recv_sem):
        self.w, self.slot = where, slot
        self.send_sem, self.recv_sem = send_sem, recv_sem
        self.sent = []

    def push(self, block, peer):
        ref = self.slot(block)
        copy = pltpu.make_async_remote_copy(
            src_ref=ref,
            dst_ref=ref,
            send_sem=self.send_sem.at[len(self.sent)],
            recv_sem=self.recv_sem.at[block],
            device_id=(self.w.dp, peer),
            device_id_type=MESH,
        )
        copy.start()
        self.sent.append(copy)

    def arrived(self, block):
        ref = self.slot(block)
        pltpu.make_async_remote_copy(
            src_ref=ref,
            dst_ref=ref,
            send_sem=self.send_sem.at[0],
            recv_sem=self.recv_sem.at[block],
            device_id=(self.w.dp, self.w.me),
            device_id_type=MESH,
        ).wait_recv()

    def start(self):
        w = self.w
        for dz in (1, LINE - 1, *range(2, LINE - 1)):
            self.push(w.me, w.at(dz, 0, False))
        self.spread(0)

    def spread(self, dz):
        w = self.w
        block = w.at(dz, 0, False)
        for dy in range(1, w.mid):
            self.push(block, w.at(0, dy, False))
        self.push(block, w.at(0, 0, True))

    def pass_on(self):
        w = self.w
        order = (1, LINE - 1, *range(2, LINE - 1))
        for dz in order:
            self.arrived(w.at(dz, 0, False))
            self.spread(dz)
        for dz in (0, *order):
            for dy in range(1, w.mid):
                self.arrived(w.at(dz, dy, False))
                self.push(w.at(dz, dy, False), w.at(0, 0, True))

    def complete(self):
        w = self.w
        for dz in (0, 1, LINE - 1, *range(2, LINE - 1)):
            for dy in range(w.mid):
                self.arrived(w.at(dz, dy, True))

    def drain(self):
        for copy in self.sent:
            copy.wait_send()


def copies_of(n_seq):
    mid = n_seq // (LINE * 2)
    return (LINE - 1) + LINE * (mid - 1) + LINE * mid


def kv_kernel(
    n_dp, n_seq, tok_ref, wk_ref, wv_ref, normed_ref, kv_ref, w_buf, w_send, w_recv, k_send, k_recv
):
    w = Where(n_dp, n_seq)
    barrier = pltpu.get_barrier_semaphore()
    near = w.near()
    for peer in near:
        pl.semaphore_signal(barrier, inc=1, device_id=(w.dp, peer), device_id_type=MESH)
    head = wk_ref.shape[1]
    w_buf[w.me, :, 0:head] = wk_ref[...]
    w_buf[w.me, :, head : 2 * head] = wv_ref[...]
    pl.semaphore_wait(barrier, len(near))
    weights = Gather(w, lambda s: w_buf.at[s], w_send, w_recv)
    weights.start()
    tok = tok_ref[...].astype(F32)
    normed = (tok * lax.rsqrt(jnp.mean(tok * tok, axis=1, keepdims=True) + 1e-06)).astype(BF16)
    normed_ref[...] = normed
    weights.pass_on()
    weights.complete()
    width = tok_ref.shape[1]
    full = merge_rows(w_buf[...], width)
    kv_ref[w.me] = jnp.dot(normed, full, preferred_element_type=F32).astype(BF16)
    blocks = Gather(w, lambda s: kv_ref.at[s], k_send, k_recv)
    blocks.start()
    blocks.pass_on()
    blocks.complete()
    weights.drain()
    blocks.drain()


def main_kernel(
    n_dp,
    n_seq,
    normed_ref,
    kv_ref,
    w_hbm,
    roww_ref,
    colw_ref,
    cot_ref,
    pair_ref,
    grow_ref,
    gcol_ref,
    wq_buf,
    wo_buf,
    att,
    feats,
    terms,
    parts,
    grads,
    turned,
    load_sem,
    f_send,
    f_recv,
    x_send,
    x_recv,
    s_send,
    r_send,
    r_recv,
    g_send,
    g_recv,
):
    w = Where(n_dp, n_seq)
    dp, me = w.dp, w.me
    every = n_dp * n_seq
    flat = dp * n_seq + me
    half = n_seq // 2
    heads_wide = wq_buf.shape[1]
    width = wq_buf.shape[0]
    load_q = pltpu.make_async_copy(w_hbm.at[:, pl.ds(0, heads_wide)], wq_buf, load_sem.at[0])
    load_o = pltpu.make_async_copy(
        w_hbm.at[:, pl.ds(heads_wide, heads_wide)], wo_buf, load_sem.at[1]
    )
    load_q.start()
    load_o.start()

    barrier = pltpu.get_barrier_semaphore()

    def greet(t, unused):
        peer = (flat + t) % every
        pl.semaphore_signal(
            barrier, inc=1, device_id=(peer // n_seq, peer % n_seq), device_id_type=MESH
        )
        return unused

    lax.fori_loop(1, every, greet, 0)

    head = kv_ref.shape[2] // 2
    rows = normed_ref.shape[0]
    length = n_seq * rows
    load_q.wait()
    queries = jnp.dot(normed_ref[...], wq_buf[...], preferred_element_type=F32).astype(BF16)
    keys = kv_ref[:, :, 0:head].reshape(length, head)
    values = kv_ref[:, :, head : 2 * head].reshape(length, head)
    factor = math.log2(math.e) / math.sqrt(head)
    for h in range(0, heads_wide // head, 2):
        both = jnp.concatenate(
            [queries[:, h * head : (h + 1) * head], queries[:, (h + 1) * head : (h + 2) * head]],
            axis=0,
        )
        scores = lax.dot_general(both, keys, LAST, preferred_element_type=F32)
        top = jnp.max(scores, axis=1, keepdims=True)
        weights = jnp.exp2((scores - top) * factor)
        total = jnp.sum(weights, axis=1, keepdims=True)
        out = jnp.dot(weights.astype(BF16), values, preferred_element_type=F32) / total
        out = out.astype(BF16)
        att[:, h * head : (h + 1) * head] = out[0:rows]
        att[:, (h + 1) * head : (h + 2) * head] = out[rows : 2 * rows]
    load_o.wait()
    update = lax.dot_general(att[...], wo_buf[...], LAST, preferred_element_type=F32)
    bins = rows // POOL
    pooled = jnp.mean(update.reshape(bins, POOL, width), axis=1)
    scale = lax.rsqrt(jnp.mean(pooled * pooled, axis=1, keepdims=True) + 1e-06)
    feat = (pooled * scale).astype(BF16)
    feats[dp, me] = feat
    pl.semaphore_wait(barrier, every - 1)

    own = Gather(w, lambda s: feats.at[dp, s], f_send, f_recv)
    own.start()
    row_proj = jnp.dot(feat, roww_ref[...], preferred_element_type=F32).astype(BF16)
    own.pass_on()

    def across(d, k):
        slot = 2 * k + w.core
        ref = feats.at[dp, slot]
        return pltpu.make_async_remote_copy(
            src_ref=ref,
            dst_ref=ref,
            send_sem=x_send.at[d, k],
            recv_sem=x_recv.at[dp, slot],
            device_id=((dp + d) % n_dp, me),
            device_id_type=MESH,
        )

    def beside(d, k, flip):
        slot = 2 * k + (1 - w.core if flip else w.core)
        other = (dp + d) % n_dp
        ref = feats.at[other, slot]
        return pltpu.make_async_remote_copy(
            src_ref=ref,
            dst_ref=ref,
            send_sem=s_send.at[d, k],
            recv_sem=x_recv.at[other, slot],
            device_id=(dp, w.at(0, 0, True)),
            device_id_type=MESH,
        )

    def each(count, act):
        def step(k, unused):
            act(k)
            return unused

        lax.fori_loop(0, count, step, 0)

    for d in range(1, n_dp):
        each(half, lambda k: across(d, k).start())
    own.complete()

    count = n_seq * bins
    mine = merge_rows(feats[dp], count)
    col_proj = jnp.dot(mine, colw_ref[...], preferred_element_type=F32).astype(BF16)
    row_wide = row_proj.astype(F32)
    col_wide = col_proj.astype(F32)
    sums = jnp.zeros(col_wide.shape, F32)
    for i in range(bins):
        sums = sums + cot_ref[i].astype(F32) * row_wide[i : i + 1, :]
    terms[...] = sums.reshape(terms.shape)

    def scatter(t):
        peer = (me + t) % n_seq
        return pltpu.make_async_remote_copy(
            src_ref=terms.at[peer],
            dst_ref=parts.at[me],
            send_sem=r_send.at[t],
            recv_sem=r_recv.at[me],
            device_id=(dp, peer),
            device_id_type=MESH,
        )

    def scattered(t):
        peer = (me + t) % n_seq
        return pltpu.make_async_remote_copy(
            src_ref=terms.at[me],
            dst_ref=parts.at[peer],
            send_sem=r_send.at[t],
            recv_sem=r_recv.at[peer],
            device_id=(dp, peer),
            device_id_type=MESH,
        )

    each(n_seq - 1, lambda k: scatter(k + 1).start())
    parts[me] = terms[me]
    row_list = []
    for i in range(bins):
        pair_ref[i] = (row_wide[i : i + 1, :] * col_wide).astype(BF16)
        row_list.append(jnp.sum(cot_ref[i].astype(F32) * col_wide, axis=0, keepdims=True))
    row_grad = jnp.concatenate(row_list, axis=0)
    each(n_seq - 1, lambda k: scattered(k + 1).wait_recv())
    col_grad = jnp.sum(parts[...], axis=0)
    grads[flat] = jnp.concatenate([row_grad, col_grad], axis=1).astype(BF16)

    def share(t):
        peer = (flat + t) % every
        return pltpu.make_async_remote_copy(
            src_ref=grads.at[flat],
            dst_ref=grads.at[flat],
            send_sem=g_send.at[t],
            recv_sem=g_recv.at[flat],
            device_id=(peer // n_seq, peer % n_seq),
            device_id_type=MESH,
        )

    def shared(t):
        peer = (flat + t) % every
        return pltpu.make_async_remote_copy(
            src_ref=grads.at[peer],
            dst_ref=grads.at[peer],
            send_sem=g_send.at[t],
            recv_sem=g_recv.at[peer],
            device_id=(dp, me),
            device_id_type=MESH,
        )

    each(every - 1, lambda k: share(k + 1).start())

    for d in range(1, n_dp):

        def relay(k):
            slot = 2 * k + w.core
            other = (dp + d) % n_dp
            ref = feats.at[other, slot]
            pltpu.make_async_remote_copy(
                src_ref=ref,
                dst_ref=ref,
                send_sem=s_send.at[d, k],
                recv_sem=x_recv.at[other, slot],
                device_id=(dp, me),
                device_id_type=MESH,
            ).wait_recv()
            beside(d, k, False).start()

        each(half, relay)
    for d in range(1, n_dp):
        each(half, lambda k: beside(d, k, True).wait_recv())
    for p in range(n_dp):
        turned[:, p * count : (p + 1) * count] = merge_rows(feats[p], count).T
    each(every - 1, lambda k: shared(k + 1).wait_recv())
    total_grad = jnp.dot(
        turned[...], merge_rows(grads[...], every * bins), preferred_element_type=F32
    ).astype(BF16)
    channels = grow_ref.shape[1]
    grow_ref[...] = total_grad[:, 0:channels]
    gcol_ref[...] = total_grad[:, channels : 2 * channels]

    own.drain()
    for d in range(1, n_dp):
        each(half, lambda k: across(d, k).wait_send())
        each(half, lambda k: beside(d, k, False).wait_send())
    each(n_seq - 1, lambda k: scatter(k + 1).wait_send())
    each(every - 1, lambda k: share(k + 1).wait_send())


def on_device(
    n_dp,
    n_seq,
    tokens,
    query_weight,
    key_weight,
    value_weight,
    output_weight,
    row_weight,
    col_weight,
    pair_cotangent,
):
    rows, width = tokens.shape[1:]
    head = key_weight.shape[1]
    heads_wide = query_weight.shape[1]
    bins, count, channels = pair_cotangent.shape[1:]
    shard = key_weight.shape[0]
    vmem = pl.BlockSpec(memory_space=pltpu.VMEM)
    dma = pltpu.SemaphoreType.DMA
    both = lax.all_gather(
        jnp.concatenate([query_weight, output_weight], axis=1), "seq", axis=0, tiled=True
    )
    moves = copies_of(n_seq)
    normed, kv = pl.pallas_call(
        functools.partial(kv_kernel, n_dp, n_seq),
        out_shape=(
            jax.ShapeDtypeStruct((rows, width), BF16),
            jax.ShapeDtypeStruct((n_seq, rows, 2 * head), BF16),
        ),
        in_specs=[vmem] * 3,
        out_specs=(vmem, vmem),
        scratch_shapes=[
            pltpu.VMEM((n_seq, shard, 2 * head), BF16),
            dma((moves,)),
            dma((n_seq,)),
            dma((moves,)),
            dma((n_seq,)),
        ],
        cost_estimate=pl.CostEstimate(
            flops=4 * rows * width * head, bytes_accessed=64 * 2**20, transcendentals=rows
        ),
        compiler_params=pltpu.CompilerParams(
            collective_id=0, has_side_effects=True, vmem_limit_bytes=24 * 2**20
        ),
    )(tokens[0], key_weight, value_weight)
    every = n_dp * n_seq
    pair, grow, gcol = pl.pallas_call(
        functools.partial(main_kernel, n_dp, n_seq),
        out_shape=(
            jax.ShapeDtypeStruct((bins, count, channels), BF16),
            jax.ShapeDtypeStruct((width, channels), BF16),
            jax.ShapeDtypeStruct((width, channels), BF16),
        ),
        in_specs=[vmem, vmem, pl.BlockSpec(memory_space=pl.ANY), vmem, vmem, vmem],
        out_specs=(vmem, vmem, vmem),
        scratch_shapes=[
            pltpu.VMEM((width, heads_wide), BF16),
            pltpu.VMEM((width, heads_wide), BF16),
            pltpu.VMEM((rows, heads_wide), BF16),
            pltpu.VMEM((n_dp, n_seq, bins, width), BF16),
            pltpu.VMEM((n_seq, bins, channels), F32),
            pltpu.VMEM((n_seq, bins, channels), F32),
            pltpu.VMEM((every, bins, 2 * channels), BF16),
            pltpu.VMEM((width, n_dp * count), BF16),
            dma((2,)),
            dma((moves,)),
            dma((n_seq,)),
            dma((n_dp, n_seq // 2)),
            dma((n_dp, n_seq)),
            dma((n_dp, n_seq // 2)),
            dma((n_seq,)),
            dma((n_seq,)),
            dma((every,)),
            dma((every,)),
        ],
        compiler_params=pltpu.CompilerParams(
            collective_id=1, has_side_effects=True, vmem_limit_bytes=60 * 2**20
        ),
    )(normed, kv, both, row_weight, col_weight, pair_cotangent[0])
    return (pair[None], grow, gcol)


def solution(mesh):
    placed = (
        P("dp", "seq", None),
        P("seq", None),
        P("seq", None),
        P("seq", None),
        P("seq", None),
        P(),
        P(),
        P("dp", "seq", None, None),
    )
    return jax.shard_map(
        functools.partial(on_device, mesh.shape["dp"], mesh.shape["seq"]),
        mesh=mesh,
        in_specs=placed,
        out_specs=(P("dp", "seq", None, None), P(), P()),
        check_vma=False,
    )
```

time: 261 us -> 123 us (0.47)
  blocking collectives: 219 us -> 0 us
  Pallas kernels: 0 us -> 64.2 us
  waiting for transfers between devices: 1.4 us -> 33.3 us
  matrix products: 19.9 us -> 0 us
  local copies, waits for them, and re-layouts: 1.08 us -> 9.39 us
    all_gather x5 -> x0, blocking collectives: 108 us -> none  [the longest x1 24.8 us: on_device(): lax.all_gather(key_weight, 'seq', axis=0, tiled=True)]
    pallas_call x0 -> x2, Pallas kernels: none -> 64.2 us  [the longest x1 34.1 us: on_device(): pl.pallas_call(functools.partial(kv_kernel, n_dp, n_seq), out_shape=(jax....]
    unnamed x1 -> x0, blocking collectives: 57.9 us -> none
    psum x1 -> x0, blocking collectives: 53.9 us -> none  [on_device(): grad_row, grad_col = lax.psum((grad_row, grad_col), ('dp', 'seq'))]
    all_gather x2 -> x1, waiting for transfers between devices: 0.02 us -> 33.3 us  [on_device(): lax.all_gather(jnp.concatenate([query_weight, output_weight], axis=1), 's...]
    dot_general x16 -> x0, matrix products: 19.9 us -> none  [the longest x4 6.17 us: attend_block(): jnp.dot(rounded, value_block, preferred_element_type=jnp.float32)]
    unnamed x13, local copies, waits for them, and re-layouts: 0.62 us -> 9.39 us
    reduce_sum x6 -> x0, other arithmetic: 2.78 us -> none  [the longest x4 1.49 us: attend_block(): run_total = run_total * factor + jnp.sum(weights, axis=1)]
  transfers between devices with their start and end apart: 2 -> 1, of which waited for: 0 -> 1; matrix products, arithmetic and copies ran while one was open for 7% -> 0% of each run, Pallas kernels for 0% -> 28%
where the time goes in v1:
time: 123 us
  Pallas kernels  64.2 us (52%)
  waiting for transfers between devices  33.3 us (27%)
  between operations  14.1 us (11%)
  local copies, waits for them, and re-layouts  9.39 us (8%)
  other arithmetic  1.79 us (1%)
    pallas_call x1, Pallas kernels, on_device(): pl.pallas_call(functools.partial(kv_kernel, n_dp, n_seq), out_shape=(jax....  34.1 us
    all_gather x1, waiting for transfers between devices, on_device(): lax.all_gather(jnp.concatenate([query_weight, output_weight], axis=1), 's...  33.3 us
    pallas_call x1, Pallas kernels, on_device(): pl.pallas_call(functools.partial(main_kernel, n_dp, n_seq), out_shape=(ja...  30.1 us
    unnamed x13, local copies, waits for them, and re-layouts  9.39 us
  transfers between devices with their start and end apart: 1, of which 1 were waited for; matrix products, arithmetic and copies ran while one was open for 0% of the time, Pallas kernels for 28%

profile of v1, /device:TPU:0, one launch (start us, length us, event | category | flops | bytes accessed | tf_op | source)
XLA Modules:
  0.0 122.8 jit_solution(299650925936200553)
XLA Ops:
  7.2 0.0 all-gather.2.cloned.1.call-start
  7.2 1.8 %pad_maximum_fusion = bf16[96,2048]{1,0:T(8,128)(2,1)} fusion(bf16[96,1024]{1,0:T(8,128)(2,1)} %param.12, bf16[96,1024]{1,0:T(8,128)(2,1)} %param.9), kind=kLoop, calls=%fused_computation | loop fusion | flops 786432 | bytes 786432 | tf_op jit(solution)/shard_map/concatenate | solution.py:399
  9.0 0.0 all-gather.2.cloned.1.call-update
  9.0 0.0 copy-start.2
  9.0 1.0 copy-done.2
  10.0 0.0 copy-start.3
  10.0 0.7 copy-done.3
  10.8 0.0 copy-start.4
  10.8 0.7 copy-done.4
  11.5 34.1 %shard_map.103 = (bf16[128,1536]{1,0:T(8,128)(2,1)S(1)}, bf16[16,128,256]{2,1,0:T(8,128)(2,1)S(1)}) custom-call(bf16[128,1536]{1,0:T(8,128)(2,1)S(1)} %bitcast.3, bf16[96,128]{1,0:T(8,128)(2,1)S(1)} %copy-done.3, bf16[96,128]{1,0:T(8,128)(2,1)S(1)} %copy-done.4), custom_call_target="tpu_custom_call" | custom-call | flops 100663296 | bytes 67108864 | tf_op jit(solution)/shard_map/pallas_call | solution.py:402
  45.7 0.0 copy-start
  45.7 1.0 copy-done
  46.6 0.0 copy-start.1
  46.7 0.7 copy-done.1
  47.4 33.3 %all-gather.2.cloned.1.call-done.w_hbm = bf16[1536,2048]{1,0:T(8,128)(2,1)} async-done(((bf16[96,2048]{1,0:T(8,128)(2,1)}), bf16[1536,2048]{1,0:T(8,128)(2,1)}) %all-gather.2.cloned.1.call-update) | async-done | bytes 6291472 | tf_op jit(solution)/shard_map/all_gather | solution.py:398
  80.7 30.1 %shard_map.104 = (bf16[8,128,128]{2,1,0:T(8,128)(2,1)}, bf16[1536,128]{1,0:T(8,128)(2,1)}, bf16[1536,128]{1,0:T(8,128)(2,1)}) custom-call(bf16[128,1536]{1,0:T(8,128)(2,1)} %copy-done.1, bf16[16,128,256]{2,1,0:T(8,128)(2,1)} %copy-done, bf16[1536,2048]{1,0:T(8,128)(2,1)} %all-gather.2.cloned.1.call-done.w_hbm, bf16[1536,128]{1,0:T(8,128)(2,1)} %roww_ref.1, ...), custom_call_target="tpu_custom_call" | custom-call | tf_op jit(solution)/shard_map/pallas_call | solution.py:425
  110.8 1.7 %copy.14 = bf16[1,8,128,128]{3,2,1,0:T(8,128)(2,1)} copy(bf16[1,8,128,128]{3,2,1,0:T(8,128)(2,1)} %bitcast.5) | data formatting | bytes 524288
  112.4 1.8 %copy.15 = bf16[1536,128]{1,0:T(8,128)(2,1)} copy(bf16[1536,128]{1,0:T(8,128)(2,1)} %get-tuple-element.17) | data formatting | bytes 786432
  114.2 1.8 %copy.16 = bf16[1536,128]{1,0:T(8,128)(2,1)} copy(bf16[1536,128]{1,0:T(8,128)(2,1)} %get-tuple-element.18) | data formatting | bytes 786432
Async XLA Ops:
  7.2 73.5 %all-gather.2.cloned.1.call-start = ((), (), s32[]{:S(2)}) async-start(), calls=%async_computation | async-start | bytes 6684672 | tf_op jit(solution)/shard_map/all_gather | solution.py:398
  9.0 1.0 copy-start.2
  10.0 0.7 copy-start.3
  10.8 0.7 copy-start.4
  45.7 1.0 copy-start
  46.6 0.7 copy-start.1
Sparse Core Ops, SparseCore 0:
  10.9 69.7 all-gather.1

commit v2 on v1

--- a/solution.py
+++ b/solution.py
@@ -10,6 +10,7 @@
 
 POOL = 16
 LINE = 4
+ORDER = (1, LINE - 1, *range(2, LINE - 1))
 F32 = jnp.float32
 BF16 = jnp.bfloat16
 MESH = pl.DeviceIdType.MESH
@@ -37,13 +38,6 @@
         core = 1 - self.core if flip else self.core
         return (z * self.mid + y) * 2 + core
 
-    def near(self):
-        return (
-            [self.at(dz, 0, False) for dz in range(1, LINE)]
-            + [self.at(0, dy, False) for dy in range(1, self.mid)]
-            + [self.at(0, 0, True)]
-        )
-
 
 class Gather:
     def __init__(self, where, slot, send_sem, recv_sem):
@@ -75,9 +69,12 @@
             device_id_type=MESH,
         ).wait_recv()
 
+    def hold(self, block):
+        pass
+
     def start(self):
         w = self.w
-        for dz in (1, LINE - 1, *range(2, LINE - 1)):
+        for dz in ORDER:
             self.push(w.me, w.at(dz, 0, False))
         self.spread(0)
 
@@ -86,22 +83,31 @@
         block = w.at(dz, 0, False)
         for dy in range(1, w.mid):
             self.push(block, w.at(0, dy, False))
+        if dz:
+            self.hold(block)
         self.push(block, w.at(0, 0, True))
 
+    def pass_line(self):
+        for dz in ORDER:
+            self.arrived(self.w.at(dz, 0, False))
+            self.spread(dz)
+
+    def pass_mid(self):
+        w = self.w
+        for dz in (0, *ORDER):
+            for dy in range(1, w.mid):
+                block = w.at(dz, dy, False)
+                self.arrived(block)
+                self.hold(block)
+                self.push(block, w.at(0, 0, True))
+
     def pass_on(self):
-        w = self.w
-        order = (1, LINE - 1, *range(2, LINE - 1))
-        for dz in order:
-            self.arrived(w.at(dz, 0, False))
-            self.spread(dz)
-        for dz in (0, *order):
-            for dy in range(1, w.mid):
-                self.arrived(w.at(dz, dy, False))
-                self.push(w.at(dz, dy, False), w.at(0, 0, True))
+        self.pass_line()
+        self.pass_mid()
 
     def complete(self):
         w = self.w
-        for dz in (0, 1, LINE - 1, *range(2, LINE - 1)):
+        for dz in (0, *ORDER):
             for dy in range(w.mid):
                 self.arrived(w.at(dz, dy, True))
 
@@ -110,62 +116,105 @@
             copy.wait_send()
 
 
+class Shared(Gather):
+    def __init__(self, where, buf, sems):
+        odd = where.dp % 2
+        super().__init__(where, lambda s: buf.at[s, pl.ds(odd, 2)], sems[0], sems[1])
+        self.buf, self.odd = buf, odd
+        self.x_send, self.x_recv, self.s_send = sems[2:]
+        self.crossed = []
+        self.beside = []
+
+    def third(self, block, piece):
+        return self.buf.at[block, piece]
+
+    def trade(self, block, piece, send_sem, dp, peer):
+        ref = self.third(block, piece)
+        return pltpu.make_async_remote_copy(
+            src_ref=ref,
+            dst_ref=ref,
+            send_sem=send_sem,
+            recv_sem=self.x_recv.at[block],
+            device_id=(dp, peer),
+            device_id_type=MESH,
+        )
+
+    def hold(self, block):
+        w = self.w
+        copy = self.trade(
+            block, 2 * self.odd, self.x_send.at[len(self.crossed)], w.dp + 1 - 2 * self.odd, w.me
+        )
+        copy.start()
+        self.crossed.append(copy)
+
+    def pass_across(self):
+        w = self.w
+        for dy in range(w.mid):
+            for dz in (0, *ORDER):
+                block = w.at(dz, dy, False)
+                send = self.s_send.at[len(self.beside)]
+                copy = self.trade(block, 2 - 2 * self.odd, send, w.dp, w.at(0, 0, True))
+                if dz or dy:
+                    copy.wait_recv()
+                copy.start()
+                self.beside.append(copy)
+
+    def complete(self):
+        super().complete()
+        w = self.w
+        for dz in (0, *ORDER):
+            for dy in range(w.mid):
+                block = w.at(dz, dy, True)
+                self.trade(
+                    block, 2 - 2 * self.odd, self.s_send.at[0], w.dp, w.at(0, 0, True)
+                ).wait_recv()
+
+    def drain(self):
+        for copy in self.sent + self.crossed + self.beside:
+            copy.wait_send()
+
+
 def copies_of(n_seq):
     mid = n_seq // (LINE * 2)
     return (LINE - 1) + LINE * (mid - 1) + LINE * mid
 
 
-def kv_kernel(
-    n_dp, n_seq, tok_ref, wk_ref, wv_ref, normed_ref, kv_ref, w_buf, w_send, w_recv, k_send, k_recv
-):
-    w = Where(n_dp, n_seq)
-    barrier = pltpu.get_barrier_semaphore()
-    near = w.near()
-    for peer in near:
-        pl.semaphore_signal(barrier, inc=1, device_id=(w.dp, peer), device_id_type=MESH)
-    head = wk_ref.shape[1]
-    w_buf[w.me, :, 0:head] = wk_ref[...]
-    w_buf[w.me, :, head : 2 * head] = wv_ref[...]
-    pl.semaphore_wait(barrier, len(near))
-    weights = Gather(w, lambda s: w_buf.at[s], w_send, w_recv)
-    weights.start()
-    tok = tok_ref[...].astype(F32)
-    normed = (tok * lax.rsqrt(jnp.mean(tok * tok, axis=1, keepdims=True) + 1e-06)).astype(BF16)
-    normed_ref[...] = normed
-    weights.pass_on()
-    weights.complete()
-    width = tok_ref.shape[1]
-    full = merge_rows(w_buf[...], width)
-    kv_ref[w.me] = jnp.dot(normed, full, preferred_element_type=F32).astype(BF16)
-    blocks = Gather(w, lambda s: kv_ref.at[s], k_send, k_recv)
-    blocks.start()
-    blocks.pass_on()
-    blocks.complete()
-    weights.drain()
-    blocks.drain()
+def shared_sems(n_seq):
+    dma = pltpu.SemaphoreType.DMA
+    half = n_seq // 2
+    return [dma((copies_of(n_seq),)), dma((n_seq,)), dma((half,)), dma((n_seq,)), dma((half,))]
 
 
 def main_kernel(
     n_dp,
     n_seq,
-    normed_ref,
-    kv_ref,
-    w_hbm,
+    tok_hbm,
+    wq_hbm,
+    wk_hbm,
+    wv_hbm,
+    wo_hbm,
+    roww_hbm,
+    colw_hbm,
+    cot_hbm,
+    rowp_ref,
+    colp_ref,
+    turned,
+    grads,
+    tok_ref,
     roww_ref,
     colw_ref,
     cot_ref,
-    pair_ref,
-    grow_ref,
-    gcol_ref,
+    wkv_buf,
     wq_buf,
     wo_buf,
+    kv_ref,
     att,
     feats,
     terms,
     parts,
-    grads,
-    turned,
     load_sem,
+    k_send,
+    k_recv,
     f_send,
     f_recv,
     x_send,
@@ -175,20 +224,32 @@
     r_recv,
     g_send,
     g_recv,
+    *weight_sems,
 ):
     w = Where(n_dp, n_seq)
     dp, me = w.dp, w.me
     every = n_dp * n_seq
     flat = dp * n_seq + me
     half = n_seq // 2
-    heads_wide = wq_buf.shape[1]
-    width = wq_buf.shape[0]
-    load_q = pltpu.make_async_copy(w_hbm.at[:, pl.ds(0, heads_wide)], wq_buf, load_sem.at[0])
-    load_o = pltpu.make_async_copy(
-        w_hbm.at[:, pl.ds(heads_wide, heads_wide)], wo_buf, load_sem.at[1]
+    head = wk_hbm.shape[2]
+    heads_wide = wq_buf.shape[3]
+    rows, width = tok_ref.shape
+
+    sources = (
+        (wk_hbm, wkv_buf.at[me, :, :, pl.ds(0, head)]),
+        (wv_hbm, wkv_buf.at[me, :, :, pl.ds(head, head)]),
+        (wq_hbm, wq_buf.at[me]),
+        (tok_hbm, tok_ref),
+        (wo_hbm, wo_buf.at[me]),
+        (roww_hbm, roww_ref),
+        (colw_hbm, colw_ref),
+        (cot_hbm, cot_ref),
     )
-    load_q.start()
-    load_o.start()
+    loads = [
+        pltpu.make_async_copy(src, dst, load_sem.at[i]) for i, (src, dst) in enumerate(sources)
+    ]
+    for load in loads:
+        load.start()
 
     barrier = pltpu.get_barrier_semaphore()
 
@@ -200,12 +261,41 @@
         return unused
 
     lax.fori_loop(1, every, greet, 0)
-
-    head = kv_ref.shape[2] // 2
-    rows = normed_ref.shape[0]
+    loads[0].wait()
+    loads[1].wait()
+    loads[2].wait()
+    pl.semaphore_wait(barrier, every - 1)
+    wkv = Shared(w, wkv_buf, weight_sems[0:5])
+    wq = Shared(w, wq_buf, weight_sems[5:10])
+    wo = Shared(w, wo_buf, weight_sems[10:15])
+    wkv.start()
+    wq.start()
+    loads[3].wait()
+    tok = tok_ref[...].astype(F32)
+    normed = (tok * lax.rsqrt(jnp.mean(tok * tok, axis=1, keepdims=True) + 1e-06)).astype(BF16)
+    wkv.pass_line()
+    wkv.pass_mid()
+    wkv.pass_across()
+    wkv.complete()
+
+    def whole(buf):
+        return merge_rows(buf[...].reshape(n_seq * 3, buf.shape[2], buf.shape[3]), width)
+
+    kv_ref[me] = jnp.dot(normed, whole(wkv_buf), preferred_element_type=F32).astype(BF16)
+    blocks = Gather(w, lambda s: kv_ref.at[s], k_send, k_recv)
+    blocks.start()
+    wq.pass_line()
+    blocks.pass_line()
+    wq.pass_mid()
+    blocks.pass_mid()
+    wq.pass_across()
+    wq.complete()
+    loads[4].wait()
+    wo.start()
+    queries = jnp.dot(normed, whole(wq_buf), preferred_element_type=F32).astype(BF16)
+    blocks.complete()
+    relays = [wo.pass_line, wo.pass_mid, wo.pass_across]
     length = n_seq * rows
-    load_q.wait()
-    queries = jnp.dot(normed_ref[...], wq_buf[...], preferred_element_type=F32).astype(BF16)
     keys = kv_ref[:, :, 0:head].reshape(length, head)
     values = kv_ref[:, :, head : 2 * head].reshape(length, head)
     factor = math.log2(math.e) / math.sqrt(head)
@@ -222,14 +312,19 @@
         out = out.astype(BF16)
         att[:, h * head : (h + 1) * head] = out[0:rows]
         att[:, (h + 1) * head : (h + 2) * head] = out[rows : 2 * rows]
-    load_o.wait()
-    update = lax.dot_general(att[...], wo_buf[...], LAST, preferred_element_type=F32)
+        if relays:
+            relays.pop(0)()
+    for relay in relays:
+        relay()
+    wo.complete()
+    update = lax.dot_general(att[...], whole(wo_buf), LAST, preferred_element_type=F32)
     bins = rows // POOL
     pooled = jnp.mean(update.reshape(bins, POOL, width), axis=1)
     scale = lax.rsqrt(jnp.mean(pooled * pooled, axis=1, keepdims=True) + 1e-06)
     feat = (pooled * scale).astype(BF16)
     feats[dp, me] = feat
-    pl.semaphore_wait(barrier, every - 1)
+    for load in loads[5:]:
+        load.wait()
 
     own = Gather(w, lambda s: feats.at[dp, s], f_send, f_recv)
     own.start()
@@ -306,9 +401,10 @@
 
     each(n_seq - 1, lambda k: scatter(k + 1).start())
     parts[me] = terms[me]
+    rowp_ref[...] = row_wide
+    colp_ref[...] = col_wide
     row_list = []
     for i in range(bins):
-        pair_ref[i] = (row_wide[i : i + 1, :] * col_wide).astype(BF16)
         row_list.append(jnp.sum(cot_ref[i].astype(F32) * col_wide, axis=0, keepdims=True))
     row_grad = jnp.concatenate(row_list, axis=0)
     each(n_seq - 1, lambda k: scattered(k + 1).wait_recv())
@@ -361,19 +457,27 @@
     for p in range(n_dp):
         turned[:, p * count : (p + 1) * count] = merge_rows(feats[p], count).T
     each(every - 1, lambda k: shared(k + 1).wait_recv())
-    total_grad = jnp.dot(
-        turned[...], merge_rows(grads[...], every * bins), preferred_element_type=F32
-    ).astype(BF16)
-    channels = grow_ref.shape[1]
-    grow_ref[...] = total_grad[:, 0:channels]
-    gcol_ref[...] = total_grad[:, channels : 2 * channels]
-
+
+    for weights in (wkv, wq, wo):
+        weights.drain()
+    blocks.drain()
     own.drain()
     for d in range(1, n_dp):
         each(half, lambda k: across(d, k).wait_send())
         each(half, lambda k: beside(d, k, False).wait_send())
     each(n_seq - 1, lambda k: scatter(k + 1).wait_send())
     each(every - 1, lambda k: share(k + 1).wait_send())
+
+
+def tail_kernel(rowp_ref, colp_ref, turned, grads, pair_ref, grow_ref, gcol_ref):
+    for i in range(rowp_ref.shape[0]):
+        pair_ref[i] = (rowp_ref[i : i + 1, :] * colp_ref[...]).astype(BF16)
+    total = jnp.dot(
+        turned[...], merge_rows(grads[...], turned.shape[1]), preferred_element_type=F32
+    ).astype(BF16)
+    channels = grow_ref.shape[1]
+    grow_ref[...] = total[:, 0:channels]
+    gcol_ref[...] = total[:, channels : 2 * channels]
 
 
 def on_device(
@@ -392,55 +496,39 @@
     head = key_weight.shape[1]
     heads_wide = query_weight.shape[1]
     bins, count, channels = pair_cotangent.shape[1:]
-    shard = key_weight.shape[0]
+    third = key_weight.shape[0] // 3
     vmem = pl.BlockSpec(memory_space=pltpu.VMEM)
+    hbm = pl.BlockSpec(memory_space=pltpu.HBM)
     dma = pltpu.SemaphoreType.DMA
-    both = lax.all_gather(
-        jnp.concatenate([query_weight, output_weight], axis=1), "seq", axis=0, tiled=True
-    )
     moves = copies_of(n_seq)
-    normed, kv = pl.pallas_call(
-        functools.partial(kv_kernel, n_dp, n_seq),
-        out_shape=(
-            jax.ShapeDtypeStruct((rows, width), BF16),
-            jax.ShapeDtypeStruct((n_seq, rows, 2 * head), BF16),
-        ),
-        in_specs=[vmem] * 3,
-        out_specs=(vmem, vmem),
-        scratch_shapes=[
-            pltpu.VMEM((n_seq, shard, 2 * head), BF16),
-            dma((moves,)),
-            dma((n_seq,)),
-            dma((moves,)),
-            dma((n_seq,)),
-        ],
-        cost_estimate=pl.CostEstimate(
-            flops=4 * rows * width * head, bytes_accessed=64 * 2**20, transcendentals=rows
-        ),
-        compiler_params=pltpu.CompilerParams(
-            collective_id=0, has_side_effects=True, vmem_limit_bytes=24 * 2**20
-        ),
-    )(tokens[0], key_weight, value_weight)
     every = n_dp * n_seq
-    pair, grow, gcol = pl.pallas_call(
+    grant = (30 if every <= 32 else 60) * 2**20
+    kept = pl.pallas_call(
         functools.partial(main_kernel, n_dp, n_seq),
         out_shape=(
-            jax.ShapeDtypeStruct((bins, count, channels), BF16),
-            jax.ShapeDtypeStruct((width, channels), BF16),
-            jax.ShapeDtypeStruct((width, channels), BF16),
+            jax.ShapeDtypeStruct((bins, channels), F32),
+            jax.ShapeDtypeStruct((count, channels), F32),
+            jax.ShapeDtypeStruct((width, n_dp * count), BF16),
+            jax.ShapeDtypeStruct((every, bins, 2 * channels), BF16),
         ),
-        in_specs=[vmem, vmem, pl.BlockSpec(memory_space=pl.ANY), vmem, vmem, vmem],
-        out_specs=(vmem, vmem, vmem),
+        in_specs=[hbm] * 8,
+        out_specs=(vmem,) * 4,
         scratch_shapes=[
-            pltpu.VMEM((width, heads_wide), BF16),
-            pltpu.VMEM((width, heads_wide), BF16),
+            pltpu.VMEM((rows, width), BF16),
+            pltpu.VMEM((width, channels), BF16),
+            pltpu.VMEM((width, channels), BF16),
+            pltpu.VMEM((bins, count, channels), BF16),
+            pltpu.VMEM((n_seq, 3, third, 2 * head), BF16),
+            pltpu.VMEM((n_seq, 3, third, heads_wide), BF16),
+            pltpu.VMEM((n_seq, 3, third, heads_wide), BF16),
+            pltpu.VMEM((n_seq, rows, 2 * head), BF16),
             pltpu.VMEM((rows, heads_wide), BF16),
             pltpu.VMEM((n_dp, n_seq, bins, width), BF16),
             pltpu.VMEM((n_seq, bins, channels), F32),
             pltpu.VMEM((n_seq, bins, channels), F32),
-            pltpu.VMEM((every, bins, 2 * channels), BF16),
-            pltpu.VMEM((width, n_dp * count), BF16),
-            dma((2,)),
+            dma((8,)),
+            dma((moves,)),
+            dma((n_seq,)),
             dma((moves,)),
             dma((n_seq,)),
             dma((n_dp, n_seq // 2)),
@@ -450,11 +538,34 @@
             dma((n_seq,)),
             dma((every,)),
             dma((every,)),
+            *shared_sems(n_seq),
+            *shared_sems(n_seq),
+            *shared_sems(n_seq),
         ],
         compiler_params=pltpu.CompilerParams(
-            collective_id=1, has_side_effects=True, vmem_limit_bytes=60 * 2**20
+            collective_id=0, has_side_effects=True, vmem_limit_bytes=grant
         ),
-    )(normed, kv, both, row_weight, col_weight, pair_cotangent[0])
+    )(
+        tokens[0],
+        query_weight.reshape(3, third, heads_wide),
+        key_weight.reshape(3, third, head),
+        value_weight.reshape(3, third, head),
+        output_weight.reshape(3, third, heads_wide),
+        row_weight,
+        col_weight,
+        pair_cotangent[0],
+    )
+    pair, grow, gcol = pl.pallas_call(
+        tail_kernel,
+        out_shape=(
+            jax.ShapeDtypeStruct((bins, count, channels), BF16),
+            jax.ShapeDtypeStruct((width, channels), BF16),
+            jax.ShapeDtypeStruct((width, channels), BF16),
+        ),
+        in_specs=[vmem] * 4,
+        out_specs=(vmem,) * 3,
+        compiler_params=pltpu.CompilerParams(vmem_limit_bytes=grant),
+    )(*kept)
     return (pair[None], grow, gcol)
 
 

time: 123 us -> 97.3 us (0.79)
  waiting for transfers between devices: 33.3 us -> 0 us
  Pallas kernels: 64.2 us -> 89 us
  between operations: 14.1 us -> 0.66 us
  local copies, waits for them, and re-layouts: 9.39 us -> 7.26 us
  other arithmetic: 1.79 us -> 0 us
    pallas_call x1, Pallas kernels: 30.1 us -> 87.7 us  [on_device(): pl.pallas_call(functools.partial(main_kernel, n_dp, n_seq), out_shape=(ja...]
    all_gather x1 -> x0, waiting for transfers between devices: 33.3 us -> none  [on_device(): lax.all_gather(jnp.concatenate([query_weight, output_weight], axis=1), 's...]
    pallas_call x1, Pallas kernels: 34.1 us -> 1.29 us  [on_device(): pl.pallas_call(tail_kernel, out_shape=(jax.ShapeDtypeStruct((bins, count,...]
    unnamed x13 -> x16, local copies, waits for them, and re-layouts: 9.39 us -> 7.26 us
    concatenate x1 -> x0, other arithmetic: 1.79 us -> none  [on_device(): jnp.concatenate([query_weight, output_weight], axis=1)]
  transfers between devices with their start and end apart: 1 -> 0, of which waited for: 1 -> 0; matrix products, arithmetic and copies ran while one was open for 0% -> 0% of each run, Pallas kernels for 28% -> 0%
where the time goes in v2:
time: 97.3 us; the launch traced here: 96.9 us
  Pallas kernels  89 us (91%)
  local copies, waits for them, and re-layouts  7.26 us (7%)
    pallas_call x1, Pallas kernels, on_device(): pl.pallas_call(functools.partial(main_kernel, n_dp, n_seq), out_shape=(ja...  87.7 us
    unnamed x16, local copies, waits for them, and re-layouts  7.26 us

profile of v2, /device:TPU:0, one launch (start us, length us, event | category | flops | bytes accessed | tf_op | source)
XLA Modules:
  0.0 96.9 jit_solution(6707428592905434659)
XLA Ops:
  0.6 0.0 copy-start
  0.6 1.0 %copy-done = bf16[1,128,1536]{2,1,0:T(8,128)(2,1)S(1)} copy-done((bf16[1,128,1536]{2,1,0:T(8,128)(2,1)S(1)}, bf16[1,128,1536]{2,1,0:T(8,128)(2,1)}, u32[]{:S(2)}) %copy-start) | copy-done | bytes 393240
  1.6 0.0 copy-start.1
  1.6 1.0 %copy-done.1 = bf16[1536,128]{1,0:T(8,128)(2,1)S(1)} copy-done((bf16[1536,128]{1,0:T(8,128)(2,1)S(1)}, bf16[1536,128]{1,0:T(8,128)(2,1)}, u32[]{:S(2)}) %copy-start.1) | copy-done | bytes 393240
  2.6 0.0 copy-start.2
  2.6 1.0 %copy-done.2 = bf16[1536,128]{1,0:T(8,128)(2,1)S(1)} copy-done((bf16[1536,128]{1,0:T(8,128)(2,1)S(1)}, bf16[1536,128]{1,0:T(8,128)(2,1)}, u32[]{:S(2)}) %copy-start.2) | copy-done | bytes 393240
  3.6 0.0 copy-start.3
  3.6 0.9 copy-done.3
  4.6 0.0 copy-start.4
  4.6 0.9 copy-done.4
  5.5 0.0 copy-start.5
  5.5 0.9 copy-done.5
  6.4 0.0 copy-start.6
  6.4 0.7 copy-done.6
  7.2 0.0 copy-start.7
  7.2 0.7 copy-done.7
  7.9 87.7 %shard_map.103 = (f32[8,128]{1,0:T(8,128)S(1)}, f32[128,128]{1,0:T(8,128)S(1)}, bf16[1536,256]{1,0:T(8,128)(2,1)S(1)}, bf16[32,8,256]{2,1,0:T(8,128)(2,1)S(1)}) custom-call(bf16[128,1536]{1,0:T(8,128)(2,1)S(1)} %bitcast.7, bf16[3,32,1024]{2,1,0:T(8,128)(2,1)S(1)} %bitcast.9, bf16[3,32,128]{2,1,0:T(8,128)(2,1)S(1)} %bitcast.11, ...), custom_call_target="tpu_custom_call" | custom-call | tf_op jit(solution)/shard_map/pallas_call | solution.py:506
  95.6 1.3 %shard_map.104 = (bf16[8,128,128]{2,1,0:T(8,128)(2,1)}, bf16[1536,128]{1,0:T(8,128)(2,1)}, bf16[1536,128]{1,0:T(8,128)(2,1)}) custom-call(f32[8,128]{1,0:T(8,128)S(1)} %get-tuple-element.10.rowp_ref, f32[128,128]{1,0:T(8,128)S(1)} %get-tuple-element.11.colp_ref, bf16[1536,256]{1,0:T(8,128)(2,1)S(1)} %get-tuple-element.12.turned, ...), custom_call_target="tpu_custom_call" | custom-call | tf_op jit(solution)/shard_map/pallas_call | solution.py:558
Async XLA Ops:
  0.6 1.0 %copy-start = (bf16[1,128,1536]{2,1,0:T(8,128)(2,1)S(1)}, bf16[1,128,1536]{2,1,0:T(8,128)(2,1)}, u32[]{:S(2)}) copy-start(bf16[1,128,1536]{2,1,0:T(8,128)(2,1)} %param.8) | copy-start | bytes 1179652
  1.6 1.0 %copy-start.1 = (bf16[1536,128]{1,0:T(8,128)(2,1)S(1)}, bf16[1536,128]{1,0:T(8,128)(2,1)}, u32[]{:S(2)}) copy-start(bf16[1536,128]{1,0:T(8,128)(2,1)} %roww_hbm.1) | copy-start | bytes 1179652
  2.6 1.0 %copy-start.2 = (bf16[1536,128]{1,0:T(8,128)(2,1)S(1)}, bf16[1536,128]{1,0:T(8,128)(2,1)}, u32[]{:S(2)}) copy-start(bf16[1536,128]{1,0:T(8,128)(2,1)} %colw_hbm.1) | copy-start | bytes 1179652
  3.6 0.9 copy-start.3
  4.6 0.9 copy-start.4
  5.5 0.9 copy-start.5
  6.4 0.7 copy-start.6
  7.2 0.7 copy-start.7

commit v3 on v2

--- a/solution.py
+++ b/solution.py
@@ -196,6 +196,10 @@
     roww_hbm,
     colw_hbm,
     cot_hbm,
+    rowp_out,
+    colp_out,
+    turned_out,
+    grads_out,
     rowp_ref,
     colp_ref,
     turned,
@@ -206,15 +210,19 @@
     cot_ref,
     wkv_buf,
     wq_buf,
-    wo_buf,
+    wo_ref,
     kv_ref,
     att,
-    feats,
+    binned,
+    pooled_ref,
     terms,
     parts,
     load_sem,
+    save_sem,
     k_send,
     k_recv,
+    b_send,
+    b_recv,
     f_send,
     f_recv,
     x_send,
@@ -230,7 +238,6 @@
     dp, me = w.dp, w.me
     every = n_dp * n_seq
     flat = dp * n_seq + me
-    half = n_seq // 2
     head = wk_hbm.shape[2]
     heads_wide = wq_buf.shape[3]
     rows, width = tok_ref.shape
@@ -240,7 +247,7 @@
         (wv_hbm, wkv_buf.at[me, :, :, pl.ds(head, head)]),
         (wq_hbm, wq_buf.at[me]),
         (tok_hbm, tok_ref),
-        (wo_hbm, wo_buf.at[me]),
+        (wo_hbm, wo_ref),
         (roww_hbm, roww_ref),
         (colw_hbm, colw_ref),
         (cot_hbm, cot_ref),
@@ -267,7 +274,6 @@
     pl.semaphore_wait(barrier, every - 1)
     wkv = Shared(w, wkv_buf, weight_sems[0:5])
     wq = Shared(w, wq_buf, weight_sems[5:10])
-    wo = Shared(w, wo_buf, weight_sems[10:15])
     wkv.start()
     wq.start()
     loads[3].wait()
@@ -290,11 +296,8 @@
     blocks.pass_mid()
     wq.pass_across()
     wq.complete()
-    loads[4].wait()
-    wo.start()
     queries = jnp.dot(normed, whole(wq_buf), preferred_element_type=F32).astype(BF16)
     blocks.complete()
-    relays = [wo.pass_line, wo.pass_mid, wo.pass_across]
     length = n_seq * rows
     keys = kv_ref[:, :, 0:head].reshape(length, head)
     values = kv_ref[:, :, head : 2 * head].reshape(length, head)
@@ -312,66 +315,82 @@
         out = out.astype(BF16)
         att[:, h * head : (h + 1) * head] = out[0:rows]
         att[:, (h + 1) * head : (h + 2) * head] = out[rows : 2 * rows]
-        if relays:
-            relays.pop(0)()
-    for relay in relays:
-        relay()
-    wo.complete()
-    update = lax.dot_general(att[...], whole(wo_buf), LAST, preferred_element_type=F32)
     bins = rows // POOL
-    pooled = jnp.mean(update.reshape(bins, POOL, width), axis=1)
-    scale = lax.rsqrt(jnp.mean(pooled * pooled, axis=1, keepdims=True) + 1e-06)
+    count = n_seq * bins
+    binned[me] = jnp.sum(att[...].astype(F32).reshape(bins, POOL, heads_wide), axis=1)
+    for load in loads[4:]:
+        load.wait()
+    attended = Gather(w, lambda s: binned.at[s], b_send, b_recv)
+    attended.start()
+    attended.pass_on()
+    attended.complete()
+    summed = binned[...].reshape(count, heads_wide)
+    high = summed.astype(BF16)
+    low = (summed - high.astype(F32)).astype(BF16)
+    update = lax.dot_general(wo_ref[...], high, LAST, preferred_element_type=F32)
+    update = update + lax.dot_general(wo_ref[...], low, LAST, preferred_element_type=F32)
+    pooled_ref[me] = update * (1.0 / POOL)
+    own = Gather(w, lambda s: pooled_ref.at[s], f_send, f_recv)
+    own.start()
+    own.pass_on()
+    own.complete()
+    pooled = pooled_ref[...].reshape(width, count)
+    scale = lax.rsqrt(jnp.mean(pooled * pooled, axis=0, keepdims=True) + 1e-06)
     feat = (pooled * scale).astype(BF16)
-    feats[dp, me] = feat
-    for load in loads[5:]:
-        load.wait()
-
-    own = Gather(w, lambda s: feats.at[dp, s], f_send, f_recv)
-    own.start()
-    row_proj = jnp.dot(feat, roww_ref[...], preferred_element_type=F32).astype(BF16)
-    own.pass_on()
-
-    def across(d, k):
-        slot = 2 * k + w.core
-        ref = feats.at[dp, slot]
+    turned[dp] = feat
+    share_rows = width // 2
+
+    def piece(p, core):
+        return turned.at[p, pl.ds(pl.multiple_of(core * share_rows, share_rows), share_rows)]
+
+    def across(d):
+        ref = piece(dp, w.core)
         return pltpu.make_async_remote_copy(
             src_ref=ref,
             dst_ref=ref,
-            send_sem=x_send.at[d, k],
-            recv_sem=x_recv.at[dp, slot],
+            send_sem=x_send.at[d],
+            recv_sem=x_recv.at[dp, w.core],
             device_id=((dp + d) % n_dp, me),
             device_id_type=MESH,
         )
 
-    def beside(d, k, flip):
-        slot = 2 * k + (1 - w.core if flip else w.core)
+    def beside(d, core):
         other = (dp + d) % n_dp
-        ref = feats.at[other, slot]
+        ref = piece(other, core)
         return pltpu.make_async_remote_copy(
             src_ref=ref,
             dst_ref=ref,
-            send_sem=s_send.at[d, k],
-            recv_sem=x_recv.at[other, slot],
+            send_sem=s_send.at[d],
+            recv_sem=x_recv.at[other, core],
             device_id=(dp, w.at(0, 0, True)),
             device_id_type=MESH,
         )
 
-    def each(count, act):
+    def each(total, act):
         def step(k, unused):
             act(k)
             return unused
 
-        lax.fori_loop(0, count, step, 0)
+        lax.fori_loop(0, total, step, 0)
 
     for d in range(1, n_dp):
-        each(half, lambda k: across(d, k).start())
-    own.complete()
-
-    count = n_seq * bins
-    mine = merge_rows(feats[dp], count)
-    col_proj = jnp.dot(mine, colw_ref[...], preferred_element_type=F32).astype(BF16)
-    row_wide = row_proj.astype(F32)
+        across(d).start()
+
+    def save(src, dst, i):
+        copy = pltpu.make_async_copy(src, dst, save_sem.at[i])
+        copy.start()
+        return copy
+
+    saves = [save(turned.at[dp], turned_out.at[dp], 0)]
+    feat_rows = feat.T
+    row_all = jnp.dot(feat_rows, roww_ref[...], preferred_element_type=F32).astype(BF16)
+    col_proj = jnp.dot(feat_rows, colw_ref[...], preferred_element_type=F32).astype(BF16)
+    rowp_ref[...] = row_all.astype(F32).reshape(rowp_ref.shape)
     col_wide = col_proj.astype(F32)
+    colp_ref[...] = col_wide
+    saves.append(save(rowp_ref.at[me], rowp_out, 1))
+    saves.append(save(colp_ref, colp_out, 2))
+    row_wide = rowp_ref[me]
     sums = jnp.zeros(col_wide.shape, F32)
     for i in range(bins):
         sums = sums + cot_ref[i].astype(F32) * row_wide[i : i + 1, :]
@@ -401,8 +420,6 @@
 
     each(n_seq - 1, lambda k: scatter(k + 1).start())
     parts[me] = terms[me]
-    rowp_ref[...] = row_wide
-    colp_ref[...] = col_wide
     row_list = []
     for i in range(bins):
         row_list.append(jnp.sum(cot_ref[i].astype(F32) * col_wide, axis=0, keepdims=True))
@@ -436,45 +453,35 @@
     each(every - 1, lambda k: share(k + 1).start())
 
     for d in range(1, n_dp):
-
-        def relay(k):
-            slot = 2 * k + w.core
-            other = (dp + d) % n_dp
-            ref = feats.at[other, slot]
-            pltpu.make_async_remote_copy(
-                src_ref=ref,
-                dst_ref=ref,
-                send_sem=s_send.at[d, k],
-                recv_sem=x_recv.at[other, slot],
-                device_id=(dp, me),
-                device_id_type=MESH,
-            ).wait_recv()
-            beside(d, k, False).start()
-
-        each(half, relay)
+        beside(d, w.core).wait_recv()
+        beside(d, w.core).start()
     for d in range(1, n_dp):
-        each(half, lambda k: beside(d, k, True).wait_recv())
-    for p in range(n_dp):
-        turned[:, p * count : (p + 1) * count] = merge_rows(feats[p], count).T
+        beside(d, 1 - w.core).wait_recv()
+        other = (dp + d) % n_dp
+        saves.append(save(turned.at[other], turned_out.at[other], 3 + d))
     each(every - 1, lambda k: shared(k + 1).wait_recv())
-
-    for weights in (wkv, wq, wo):
+    saves.append(save(grads, grads_out, 3))
+    for weights in (wkv, wq, blocks, attended, own):
         weights.drain()
-    blocks.drain()
-    own.drain()
     for d in range(1, n_dp):
-        each(half, lambda k: across(d, k).wait_send())
-        each(half, lambda k: beside(d, k, False).wait_send())
+        across(d).wait_send()
+        beside(d, w.core).wait_send()
     each(n_seq - 1, lambda k: scatter(k + 1).wait_send())
     each(every - 1, lambda k: share(k + 1).wait_send())
+    for copy in saves:
+        copy.wait()
 
 
 def tail_kernel(rowp_ref, colp_ref, turned, grads, pair_ref, grow_ref, gcol_ref):
     for i in range(rowp_ref.shape[0]):
         pair_ref[i] = (rowp_ref[i : i + 1, :] * colp_ref[...]).astype(BF16)
-    total = jnp.dot(
-        turned[...], merge_rows(grads[...], turned.shape[1]), preferred_element_type=F32
-    ).astype(BF16)
+    n_dp, width, count = turned.shape
+    whole = merge_rows(grads[...], n_dp * count)
+    total = jnp.zeros((width, whole.shape[1]), F32)
+    for p in range(n_dp):
+        part = whole[p * count : (p + 1) * count]
+        total = total + jnp.dot(turned[p], part, preferred_element_type=F32)
+    total = total.astype(BF16)
     channels = grow_ref.shape[1]
     grow_ref[...] = total[:, 0:channels]
     gcol_ref[...] = total[:, channels : 2 * channels]
@@ -502,43 +509,45 @@
     dma = pltpu.SemaphoreType.DMA
     moves = copies_of(n_seq)
     every = n_dp * n_seq
-    grant = (30 if every <= 32 else 60) * 2**20
+    grant = 60 * 2**20
     kept = pl.pallas_call(
         functools.partial(main_kernel, n_dp, n_seq),
         out_shape=(
             jax.ShapeDtypeStruct((bins, channels), F32),
             jax.ShapeDtypeStruct((count, channels), F32),
-            jax.ShapeDtypeStruct((width, n_dp * count), BF16),
+            jax.ShapeDtypeStruct((n_dp, width, count), BF16),
             jax.ShapeDtypeStruct((every, bins, 2 * channels), BF16),
         ),
         in_specs=[hbm] * 8,
-        out_specs=(vmem,) * 4,
+        out_specs=(hbm,) * 4,
         scratch_shapes=[
+            pltpu.VMEM((n_seq, bins, channels), F32),
+            pltpu.VMEM((count, channels), F32),
+            pltpu.VMEM((n_dp, width, count), BF16),
+            pltpu.VMEM((every, bins, 2 * channels), BF16),
             pltpu.VMEM((rows, width), BF16),
             pltpu.VMEM((width, channels), BF16),
             pltpu.VMEM((width, channels), BF16),
             pltpu.VMEM((bins, count, channels), BF16),
             pltpu.VMEM((n_seq, 3, third, 2 * head), BF16),
             pltpu.VMEM((n_seq, 3, third, heads_wide), BF16),
-            pltpu.VMEM((n_seq, 3, third, heads_wide), BF16),
+            pltpu.VMEM(output_weight.shape, BF16),
             pltpu.VMEM((n_seq, rows, 2 * head), BF16),
             pltpu.VMEM((rows, heads_wide), BF16),
-            pltpu.VMEM((n_dp, n_seq, bins, width), BF16),
+            pltpu.VMEM((n_seq, bins, heads_wide), F32),
+            pltpu.VMEM((n_seq, 3 * third, count), F32),
             pltpu.VMEM((n_seq, bins, channels), F32),
             pltpu.VMEM((n_seq, bins, channels), F32),
             dma((8,)),
-            dma((moves,)),
-            dma((n_seq,)),
-            dma((moves,)),
-            dma((n_seq,)),
-            dma((n_dp, n_seq // 2)),
-            dma((n_dp, n_seq)),
-            dma((n_dp, n_seq // 2)),
+            dma((3 + n_dp,)),
+            *[dma((moves,)), dma((n_seq,))] * 3,
+            dma((n_dp,)),
+            dma((n_dp, 2)),
+            dma((n_dp,)),
             dma((n_seq,)),
             dma((n_seq,)),
             dma((every,)),
             dma((every,)),
-            *shared_sems(n_seq),
             *shared_sems(n_seq),
             *shared_sems(n_seq),
         ],
@@ -550,7 +559,7 @@
         query_weight.reshape(3, third, heads_wide),
         key_weight.reshape(3, third, head),
         value_weight.reshape(3, third, head),
-        output_weight.reshape(3, third, heads_wide),
+        output_weight,
         row_weight,
         col_weight,
         pair_cotangent[0],

time: 97.3 us -> 79 us (0.81)
  Pallas kernels: 89 us -> 78.2 us
  local copies, waits for them, and re-layouts: 7.26 us -> 0 us
    pallas_call x1, Pallas kernels: 87.7 us -> 75.6 us  [on_device(): pl.pallas_call(functools.partial(main_kernel, n_dp, n_seq), out_shape=(ja...]
    unnamed x16 -> x0, local copies, waits for them, and re-layouts: 7.26 us -> none
    pallas_call x1, Pallas kernels: 1.29 us -> 2.67 us  [on_device(): pl.pallas_call(tail_kernel, out_shape=(jax.ShapeDtypeStruct((bins, count,...]
where the time goes in v3:
time: 79 us; the launch traced here: 78.9 us
  Pallas kernels  78.2 us (99%)
    pallas_call x1, Pallas kernels, on_device(): pl.pallas_call(functools.partial(main_kernel, n_dp, n_seq), out_shape=(ja...  75.6 us
    pallas_call x1, Pallas kernels, on_device(): pl.pallas_call(tail_kernel, out_shape=(jax.ShapeDtypeStruct((bins, count,...  2.67 us

profile of v3, /device:TPU:0, one launch (start us, length us, event | category | flops | bytes accessed | tf_op | source)
XLA Modules:
  0.0 78.9 jit_solution(11619610332967978784)
XLA Ops:
  0.6 75.6 %shard_map.103 = (f32[8,128]{1,0:T(8,128)}, f32[128,128]{1,0:T(8,128)}, bf16[2,1536,128]{2,1,0:T(8,128)(2,1)}, bf16[32,8,256]{2,1,0:T(8,128)(2,1)}) custom-call(bf16[128,1536]{1,0:T(8,128)(2,1)} %bitcast.6, bf16[3,32,1024]{2,1,0:T(8,128)(2,1)} %bitcast.8, bf16[3,32,128]{2,1,0:T(8,128)(2,1)} %bitcast.9, bf16[3,32,128]{2,1,0:T(8,128)(2,1)} %bitcast.10, ...), custom_call_target="tpu_custom_call" | custom-call | tf_op jit(solution)/shard_map/pallas_call | solution.py:513
  76.2 2.7 %shard_map.104 = (bf16[8,128,128]{2,1,0:T(8,128)(2,1)}, bf16[1536,128]{1,0:T(8,128)(2,1)}, bf16[1536,128]{1,0:T(8,128)(2,1)}) custom-call(f32[8,128]{1,0:T(8,128)} %get-tuple-element.10.rowp_ref, f32[128,128]{1,0:T(8,128)} %get-tuple-element.11.colp_ref, bf16[2,1536,128]{2,1,0:T(8,128)(2,1)} %get-tuple-element.12.turned, ...), custom_call_target="tpu_custom_call" | custom-call | tf_op jit(solution)/shard_map/pallas_call | solution.py:567

commit v4 on v3

--- a/solution.py
+++ b/solution.py
@@ -272,8 +272,8 @@
     loads[1].wait()
     loads[2].wait()
     pl.semaphore_wait(barrier, every - 1)
-    wkv = Shared(w, wkv_buf, weight_sems[0:5])
-    wq = Shared(w, wq_buf, weight_sems[5:10])
+    wkv = Gather(w, lambda s: wkv_buf.at[s], weight_sems[0], weight_sems[1])
+    wq = Shared(w, wq_buf, weight_sems[2:7])
     wkv.start()
     wq.start()
     loads[3].wait()
@@ -281,7 +281,6 @@
     normed = (tok * lax.rsqrt(jnp.mean(tok * tok, axis=1, keepdims=True) + 1e-06)).astype(BF16)
     wkv.pass_line()
     wkv.pass_mid()
-    wkv.pass_across()
     wkv.complete()
 
     def whole(buf):
@@ -373,9 +372,6 @@
 
         lax.fori_loop(0, total, step, 0)
 
-    for d in range(1, n_dp):
-        across(d).start()
-
     def save(src, dst, i):
         copy = pltpu.make_async_copy(src, dst, save_sem.at[i])
         copy.start()
@@ -419,6 +415,9 @@
         )
 
     each(n_seq - 1, lambda k: scatter(k + 1).start())
+    for d in range(1, n_dp):
+        across(d).start()
+
     parts[me] = terms[me]
     row_list = []
     for i in range(bins):
@@ -548,7 +547,7 @@
             dma((n_seq,)),
             dma((every,)),
             dma((every,)),
-            *shared_sems(n_seq),
+            *shared_sems(n_seq)[:2],
             *shared_sems(n_seq),
         ],
         compiler_params=pltpu.CompilerParams(

time: 79 us -> 78 us (0.987)
  Pallas kernels: 78.2 us -> 77.2 us
    pallas_call x1, Pallas kernels: 75.6 us -> 74.5 us  [on_device(): pl.pallas_call(functools.partial(main_kernel, n_dp, n_seq), out_shape=(ja...]
where the time goes in v4:
time: 78 us; the launch traced here: 77.8 us
  Pallas kernels  77.2 us (99%)
    pallas_call x1, Pallas kernels, on_device(): pl.pallas_call(functools.partial(main_kernel, n_dp, n_seq), out_shape=(ja...  74.5 us
    pallas_call x1, Pallas kernels, on_device(): pl.pallas_call(tail_kernel, out_shape=(jax.ShapeDtypeStruct((bins, count,...  2.66 us

profile of v4, /device:TPU:0, one launch (start us, length us, event | category | flops | bytes accessed | tf_op | source)
XLA Modules:
  0.0 77.8 jit_solution(15204837232814270076)
XLA Ops:
  0.6 74.5 %shard_map.103 = (f32[8,128]{1,0:T(8,128)}, f32[128,128]{1,0:T(8,128)}, bf16[2,1536,128]{2,1,0:T(8,128)(2,1)}, bf16[32,8,256]{2,1,0:T(8,128)(2,1)}) custom-call(bf16[128,1536]{1,0:T(8,128)(2,1)} %bitcast.6, bf16[3,32,1024]{2,1,0:T(8,128)(2,1)} %bitcast.8, bf16[3,32,128]{2,1,0:T(8,128)(2,1)} %bitcast.9, bf16[3,32,128]{2,1,0:T(8,128)(2,1)} %bitcast.10, ...), custom_call_target="tpu_custom_call" | custom-call | tf_op jit(solution)/shard_map/pallas_call | solution.py:512
  75.1 2.7 %shard_map.104 = (bf16[8,128,128]{2,1,0:T(8,128)(2,1)}, bf16[1536,128]{1,0:T(8,128)(2,1)}, bf16[1536,128]{1,0:T(8,128)(2,1)}) custom-call(f32[8,128]{1,0:T(8,128)} %get-tuple-element.10.rowp_ref, f32[128,128]{1,0:T(8,128)} %get-tuple-element.11.colp_ref, bf16[2,1536,128]{2,1,0:T(8,128)(2,1)} %get-tuple-element.12.turned, ...), custom_call_target="tpu_custom_call" | custom-call | tf_op jit(solution)/shard_map/pallas_call | solution.py:566
